TPU v7x, 32 devices: a whole 2x2x4 slice. The times are simulated.
32 devices in a mesh: ctx: 8 (over z, y), grp: 4 (over x, core).
Axes of the slice: x: 2, y: 2, z: 4, core: 2. Of those that a mesh axis runs over, the one named last changes fastest.
Arguments:
- streams: bfloat16 [3, 3072, 4096], P(None, 'ctx', 'grp'), may hold values from -400 to 400
- filters: bfloat16 [3, 256, 128], P(None, 'grp'), may hold values from -0.5 to 0.5
- gain: float32 [4096], P('grp'), may hold values from 0.5 to 1.5
Outputs:
- normed: bfloat16 [3072, 4096], P('ctx', 'grp')
All inputs are finite; a program needn't handle non-finite values.
Results may differ from a plain program's by a relative error of at most 0.012.
The roundings to bfloat16 on the way count: a program that leaves them out, or rounds other values in their place, can miss the bound.
Values may be sent and summed in bfloat16 or wider, within the bound.
A program may use at most 128 MiB of HBM per device.

v0:
```python
import math
import jax
import jax.numpy as jnp
import numpy as np
from jax import lax
from jax.sharding import PartitionSpec as P

HD = 128
CH = 4096


def passed_along(block, axis, distance):
    devices = range(lax.axis_size(axis))
    route = [(i - distance, i) for i in devices if i - distance in devices]
    return lax.ppermute(block, axis, route)


def filter_all(streams, filters):
    tok_rows = streams.shape[1]
    chan_count = streams.shape[2]
    filt_len = filters.shape[2]
    group_count = filters.shape[1]
    group_width = chan_count // group_count
    tail = streams[:, tok_rows - filt_len :, :]
    before = passed_along(tail, "ctx", 1)
    padded = jnp.concatenate([before, streams], axis=1)
    block_count = tok_rows // filt_len
    blocks = padded.reshape(3, block_count + 1, filt_len, group_count, group_width)
    lag_table = np.arange(filt_len)[:, None] - np.arange(filt_len)[None, :]
    lower_idx = np.where(lag_table >= 0, lag_table, 0)
    upper_idx = np.where(lag_table < 0, lag_table + filt_len, 0)
    lower = jnp.where(lag_table >= 0, filters[:, :, lower_idx], 0.0)
    upper = jnp.where(lag_table < 0, filters[:, :, upper_idx], 0.0)
    result = jnp.einsum(
        "agts,absgc->abtgc", lower, blocks[:, 1:], preferred_element_type=jnp.float32
    )
    result = result + jnp.einsum(
        "agts,absgc->abtgc", upper, blocks[:, :-1], preferred_element_type=jnp.float32
    )
    return result.reshape(3, tok_rows, chan_count).astype(jnp.bfloat16)


def attend(queries, positions, keyed, valued):
    tok_rows, chan_count = queries.shape
    head_count = chan_count // HD
    scale = HD ** (-0.5)
    query_heads = queries.reshape(tok_rows, head_count, HD)
    query_last = jnp.max(positions)
    start_state = (
        jnp.full((head_count, tok_rows), -1e30, jnp.float32),
        jnp.zeros((head_count, tok_rows), jnp.float32),
        jnp.zeros((tok_rows, head_count, HD), jnp.float32),
    )
    key_piece = lax.all_gather(keyed, "ctx", axis=0, tiled=True)
    value_piece = lax.all_gather(valued, "ctx", axis=0, tiled=True)
    piece_len = key_piece.shape[0]
    block_len = math.gcd(piece_len, 512)

    def step_block(step_idx, state):
        offset = step_idx * block_len
        key_block = lax.dynamic_slice_in_dim(key_piece, offset, block_len, 0).reshape(
            block_len, head_count, HD
        )
        value_block = lax.dynamic_slice_in_dim(value_piece, offset, block_len, 0).reshape(
            block_len, head_count, HD
        )
        key_pos = offset + jnp.arange(block_len, dtype=jnp.int32)

        def update_block(inner):
            running, totals, accum = inner
            scores = (
                jnp.einsum(
                    "shd,khd->hsk", query_heads, key_block, preferred_element_type=jnp.float32
                )
                * scale
            )
            causal = key_pos[None, None, :] <= positions[None, :, None]
            newtop = jnp.maximum(running, jnp.max(jnp.where(causal, scores, -1e30), axis=2))
            weights = jnp.where(causal, jnp.exp(scores - newtop[:, :, None]), 0.0)
            factor = jnp.exp(running - newtop)
            totals = totals * factor + jnp.sum(weights, axis=2)
            accum = accum * factor.T[:, :, None] + jnp.einsum(
                "hsk,khd->shd",
                weights.astype(jnp.bfloat16),
                value_block,
                preferred_element_type=jnp.float32,
            )
            return (newtop, totals, accum)

        return lax.cond(offset > query_last, lambda inner: inner, update_block, state)

    running, totals, accum = lax.fori_loop(0, piece_len // block_len, step_block, start_state)
    return (accum / totals.T[:, :, None]).reshape(tok_rows, chan_count).astype(jnp.bfloat16)


def local(streams, filters, gain):
    features = filter_all(streams, filters)
    tok_rows = streams.shape[1]
    my_index = lax.axis_index("ctx")
    queries = features[0]
    positions = my_index * tok_rows + jnp.arange(tok_rows, dtype=jnp.int32)
    attended = attend(queries, positions, features[1], features[2])
    wide = attended.astype(jnp.float32)
    power = lax.psum(jnp.sum(wide * wide, axis=1), "grp") / CH
    return (wide * gain[None, :] * lax.rsqrt(power + 1e-06)[:, None]).astype(jnp.bfloat16)


def solution(mesh):
    placed = (P(None, "ctx", "grp"), P(None, "grp", None), P("grp"))
    return jax.shard_map(
        local, mesh=mesh, in_specs=placed, out_specs=P("ctx", "grp"), check_vma=False
    )
```

profile of v0, /device:TPU:24, one launch (start us, length us, event | category | flops | bytes accessed | tf_op | source)
XLA Modules:
  0.0 568.2 jit_solution(7154377040794997620)
XLA Ops:
  6.5 1.2 slice.21
  7.7 3.4 collective-permute-start
  13.0 112.9 %gather_fusion.1 = bf16[16384,3,64]{2,1,0:T(4,128)(2,1)} fusion(bf16[3,64,128]{1,0,2:T(4,128)(2,1)S(1)} %copy.17, s32[16384]{0:T(1024)S(1)} %broadcast_clamp_fusion), kind=kCustom, calls=%fused_computation.1 | custom fusion | bytes 12648448 | tf_op jit(solution)/shard_map/gather | solution.py:33
  125.9 17.2 %copy.21 = bf16[128,128,3,64]{1,0,3,2:T(8,128)(2,1)} copy(bf16[128,128,3,64]{3,2,1,0:T(4,128)(2,1)} %bitcast.81) | data formatting | bytes 12582912 | tf_op jit(solution)/shard_map/gather | solution.py:33
  143.1 112.7 %gather_fusion = bf16[16384,3,64]{2,1,0:T(4,128)(2,1)} fusion(bf16[3,64,128]{1,0,2:T(4,128)(2,1)S(1)} %copy.17, s32[16384]{0:T(1024)S(1)} %broadcast_clamp_fusion.1), kind=kCustom, calls=%fused_computation | custom fusion | bytes 12648448 | tf_op jit(solution)/shard_map/gather | solution.py:32
  255.9 17.2 %copy.18 = bf16[128,128,3,64]{1,0,3,2:T(8,128)(2,1)} copy(bf16[128,128,3,64]{3,2,1,0:T(4,128)(2,1)} %bitcast.80) | data formatting | bytes 12582912 | tf_op jit(solution)/shard_map/gather | solution.py:32
  273.1 2.1 pad_maximum_fusion
  275.2 3.0 copy.15
  278.2 5.7 %reshape.74 = bf16[3,4,128,64,16]{2,1,4,3,0:T(4,128)(2,1)} reshape(bf16[3,512,1024]{1,2,0:T(8,128)(2,1)} %copy.15) | data formatting | bytes 6291456 | tf_op jit(solution)/shard_map/reshape | solution.py:28
  283.9 8.0 %fusion.40 = (bf16[3,3,128,64,16]{2,1,4,3,0:T(4,128)(2,1)}, bf16[3,3,128,64,16]{2,1,4,3,0:T(4,128)(2,1)S(1)}) fusion(bf16[3,4,128,64,16]{2,1,4,3,0:T(4,128)(2,1)} %reshape.74), kind=kLoop, calls=%fused_computation.56 | loop fusion | bytes 9437184 | tf_op jit(solution)/shard_map/slice | solution.py:35
  292.0 6.0 %fusion.18 = f32[3,64,3,16,128]{4,3,2,1,0:T(8,128)} fusion(bf16[128,128,3,64]{1,0,3,2:T(8,128)(2,1)S(1)} %bitcast.79, pred[128,128]{1,0:T(8,128)(4,1)S(1)} %bitcast.89, bf16[3,3,128,64,16]{2,1,4,3,0:T(4,128)(2,1)S(1)} %get-tuple-element.351), kind=kOutput, calls=%fused_computation.26 | convolution fusion | flops 305135616 | bytes 13385728 | tf_op jit(solution)/shard_map/agts,absgc->abtgc/dot_general | solution.py:37
  298.1 7.8 %fusion.28 = bf16[3,3,128,64,16]{2,4,1,3,0:T(8,128)(2,1)S(1)} fusion(f32[3,64,3,16,128]{4,3,2,1,0:T(8,128)} %fusion.18, bf16[128,128,3,64]{1,0,3,2:T(8,128)(2,1)S(1)} %bitcast.77, pred[128,128]{1,0:T(8,128)(4,1)S(1)} %bitcast.88, bf16[3,3,128,64,16]{2,1,4,3,0:T(4,128)(2,1)} %get-tuple-element.350), kind=kOutput, calls=%fused_computation.38 | convolution fusion | flops 307494912 | bytes 15745024 | tf_op jit(solution)/shard_map/agts,absgc->abtgc/dot_general | solution.py:34
  308.6 1.1 copy.46
  312.0 93.6 %all-gather.3.cloned.1.call-done = bf16[3072,1024]{0,1:T(8,128)(2,1)} async-done(((bf16[384,1024]{0,1:T(8,128)(2,1)}), bf16[3072,1024]{0,1:T(8,128)(2,1)}) %all-gather.3.cloned.1.call-update) | async-done | bytes 6291472 | tf_op jit(solution)/shard_map/all_gather | solution.py:54
  405.6 99.8 %all-gather.5.cloned.1.call-done = bf16[3072,1024]{0,1:T(8,128)(2,1)} async-done(((bf16[384,1024]{0,1:T(8,128)(2,1)}), bf16[3072,1024]{0,1:T(8,128)(2,1)}) %all-gather.5.cloned.1.call-update) | async-done | bytes 6291472 | tf_op jit(solution)/shard_map/all_gather | solution.py:55
  505.5 47.3 %while.18 = (s32[]{:T(128)}, f32[8,384]{1,0:T(8,128)S(1)}, f32[8,384]{1,0:T(8,128)S(1)}, f32[384,8,128]{2,0,1:T(8,128)S(1)}, s32[]{:T(128)}, /*index=5*/bf16[307...) while((s32[]{:T(128)}, f32[8,384]{1,0:T(8,128)S(1)}, ...), condition=%wide.region_6.7_spmd.clone, body=%wide.region_1.6_spmd.clone.sunk | while | flops 823601024 | bytes 30095668 | solution.py:92
  506.2 7.3 %conditional.3 = (f32[8,384]{1,0:T(8,128)S(1)}, f32[8,384]{1,0:T(8,128)S(1)}, f32[384,8,128]{2,0,1:T(8,128)S(1)}) conditional(s32[]{:T(128)} %convert_element_type.65, (s32[]{:T(128)}, s32[512]{0:T(512)S(1)}, s32[]{:T(128)}, bf16[3072,1024]{0,1:T(8,128)(2,1)}, bf16[384,8,128]{2,0,1:T(8,128)(2,1)S(1)}, /*index=5*/f32[8,384]{1,0:T(8,128)S(1)}, ...), branch_computations={%region_2.4_spmd, %region_5.5_spmd} | conditional | flops 823601024 | bytes 30067270 | solution.py:90
  506.2 1.7 constant_dynamic-slice_fusion
  508.1 1.5 fusion.2
  509.6 2.5 bitcast_add_fusion
  512.1 1.3 fusion.6
  514.0 7.3 %conditional.3 = (f32[8,384]{1,0:T(8,128)S(1)}, f32[8,384]{1,0:T(8,128)S(1)}, f32[384,8,128]{2,0,1:T(8,128)S(1)}) conditional(s32[]{:T(128)} %convert_element_type.65, (s32[]{:T(128)}, s32[512]{0:T(512)S(1)}, s32[]{:T(128)}, bf16[3072,1024]{0,1:T(8,128)(2,1)}, bf16[384,8,128]{2,0,1:T(8,128)(2,1)S(1)}, /*index=5*/f32[8,384]{1,0:T(8,128)S(1)}, ...), branch_computations={%region_2.4_spmd, %region_5.5_spmd} | conditional | flops 823601024 | bytes 30067270 | solution.py:90
  514.1 1.7 constant_dynamic-slice_fusion
  516.0 1.5 fusion.2
  517.5 2.5 bitcast_add_fusion
  520.0 1.3 fusion.6
  521.9 7.3 %conditional.3 = (f32[8,384]{1,0:T(8,128)S(1)}, f32[8,384]{1,0:T(8,128)S(1)}, f32[384,8,128]{2,0,1:T(8,128)S(1)}) conditional(s32[]{:T(128)} %convert_element_type.65, (s32[]{:T(128)}, s32[512]{0:T(512)S(1)}, s32[]{:T(128)}, bf16[3072,1024]{0,1:T(8,128)(2,1)}, bf16[384,8,128]{2,0,1:T(8,128)(2,1)S(1)}, /*index=5*/f32[8,384]{1,0:T(8,128)S(1)}, ...), branch_computations={%region_2.4_spmd, %region_5.5_spmd} | conditional | flops 823601024 | bytes 30067270 | solution.py:90
  521.9 1.7 constant_dynamic-slice_fusion
  523.8 1.5 fusion.2
  525.4 2.5 bitcast_add_fusion
  527.8 1.3 fusion.6
  529.8 7.3 %conditional.3 = (f32[8,384]{1,0:T(8,128)S(1)}, f32[8,384]{1,0:T(8,128)S(1)}, f32[384,8,128]{2,0,1:T(8,128)S(1)}) conditional(s32[]{:T(128)} %convert_element_type.65, (s32[]{:T(128)}, s32[512]{0:T(512)S(1)}, s32[]{:T(128)}, bf16[3072,1024]{0,1:T(8,128)(2,1)}, bf16[384,8,128]{2,0,1:T(8,128)(2,1)S(1)}, /*index=5*/f32[8,384]{1,0:T(8,128)S(1)}, ...), branch_computations={%region_2.4_spmd, %region_5.5_spmd} | conditional | flops 823601024 | bytes 30067270 | solution.py:90
  529.8 1.7 constant_dynamic-slice_fusion
  531.7 1.5 fusion.2
  533.2 2.5 bitcast_add_fusion
  535.7 1.3 fusion.6
  537.7 7.3 %conditional.3 = (f32[8,384]{1,0:T(8,128)S(1)}, f32[8,384]{1,0:T(8,128)S(1)}, f32[384,8,128]{2,0,1:T(8,128)S(1)}) conditional(s32[]{:T(128)} %convert_element_type.65, (s32[]{:T(128)}, s32[512]{0:T(512)S(1)}, s32[]{:T(128)}, bf16[3072,1024]{0,1:T(8,128)(2,1)}, bf16[384,8,128]{2,0,1:T(8,128)(2,1)S(1)}, /*index=5*/f32[8,384]{1,0:T(8,128)S(1)}, ...), branch_computations={%region_2.4_spmd, %region_5.5_spmd} | conditional | flops 823601024 | bytes 30067270 | solution.py:90
  537.7 1.7 constant_dynamic-slice_fusion
  539.6 1.5 fusion.2
  541.1 2.5 bitcast_add_fusion
  543.6 1.3 fusion.6
  545.6 7.3 %conditional.3 = (f32[8,384]{1,0:T(8,128)S(1)}, f32[8,384]{1,0:T(8,128)S(1)}, f32[384,8,128]{2,0,1:T(8,128)S(1)}) conditional(s32[]{:T(128)} %convert_element_type.65, (s32[]{:T(128)}, s32[512]{0:T(512)S(1)}, s32[]{:T(128)}, bf16[3072,1024]{0,1:T(8,128)(2,1)}, bf16[384,8,128]{2,0,1:T(8,128)(2,1)S(1)}, /*index=5*/f32[8,384]{1,0:T(8,128)S(1)}, ...), branch_computations={%region_2.4_spmd, %region_5.5_spmd} | conditional | flops 823601024 | bytes 30067270 | solution.py:90
  545.6 1.7 constant_dynamic-slice_fusion
  547.5 1.5 fusion.2
  549.0 2.5 bitcast_add_fusion
  551.5 1.3 fusion.6
  553.4 6.8 %psum.7 = f32[384]{0:T(512)S(1)} all-reduce(f32[384]{0:T(512)S(1)} %get-tuple-element.344), channel_id=1, replica_groups=mesh['ctx'=8,'grp'=4] {'grp'}, use_global_device_ids=true, to_apply=%region_8.9 | all-reduce | flops 384 | bytes 3072 | tf_op jit(solution)/shard_map/psum | solution.py:104
  560.3 1.1 fusion.37
  (87 shorter events, 8.8 us)
Async XLA Ops:
  6.5 399.1 %all-gather.3.cloned.1.call-start = ((), (), s32[]{:S(2)}) async-start(), calls=%async_computation | async-start | bytes 7077888 | tf_op jit(solution)/shard_map/all_gather | solution.py:54
  7.7 265.4 %collective-permute-start = (bf16[3,128,1024]{2,1,0:T(8,128)(2,1)S(1)}, bf16[3,128,1024]{2,1,0:T(8,128)(2,1)}, u32[]{:S(2)}, u32[]{:S(2)}) collective-permute-start(bf16[3,128,1024]{2,1,0:T(8,128)(2,1)S(1)} %slice.21), channel_id=1, source_target_pairs={{0,4},{4,8},{8,12},{12,16},{16,20},{20,24},{24,28},{1,5},{5,9},{9,... | collective-permute-start | bytes 2359304 | tf_op jit(solution)/shard_map/ppermute | solution.py:15
  125.9 17.3 %copy-start.2 = (s32[16384]{0:T(1024)S(1)}, s32[16384]{0:T(1024)}, u32[]{:S(2)}) copy-start(s32[16384]{0:T(1024)} %constant.103) | copy-start | bytes 196612
  278.2 13.7 %slice-start.2 = ((s8[6291456]{0:T(1024)(128)(4,1)}), s8[2097152]{0:T(1024)(128)(4,1)S(1)}, s32[]{:S(2)}) async-start(s8[6291456]{0:T(1024)(128)(4,1)} %bitcast.78), calls=%async_computation.4 | async-start | bytes 4194304
  283.9 8.1 %slice-start.3 = ((s8[6291456]{0:T(1024)(128)(4,1)}), s8[4194304]{0:T(1024)(128)(4,1)S(1)}, s32[]{:S(2)}) async-start(s8[6291456]{0:T(1024)(128)(4,1)} %bitcast.78), calls=%async_computation.5 | async-start | bytes 8388608
  283.9 8.1 %copy-start.1 = (pred[128,128]{1,0:T(32,128)(4,1)S(1)}, pred[128,128]{1,0:T(32,128)(4,1)}, u32[]{:S(2)}) copy-start(pred[128,128]{1,0:T(32,128)(4,1)} %constant.100.clone) | copy-start | bytes 49156
  283.9 14.1 %slice-start = ((s8[6291456]{0:T(1024)(128)(4,1)}), s8[4194304]{0:T(1024)(128)(4,1)S(1)}, s32[]{:S(2)}) async-start(s8[6291456]{0:T(1024)(128)(4,1)} %bitcast.76), calls=%async_computation.2 | async-start | bytes 8388608
  292.0 6.1 %slice-start.1 = ((s8[6291456]{0:T(1024)(128)(4,1)}), s8[2097152]{0:T(1024)(128)(4,1)S(1)}, s32[]{:S(2)}) async-start(s8[6291456]{0:T(1024)(128)(4,1)} %bitcast.76), calls=%async_computation.3 | async-start | bytes 4194304
  292.0 6.1 %copy-start = (pred[128,128]{1,0:T(32,128)(4,1)S(1)}, pred[128,128]{1,0:T(32,128)(4,1)}, u32[]{:S(2)}) copy-start(pred[128,128]{1,0:T(32,128)(4,1)} %constant.98.clone) | copy-start | bytes 49156
  307.9 197.5 %all-gather.5.cloned.1.call-start = ((), (), s32[]{:S(2)}) async-start(), calls=%async_computation.1 | async-start | bytes 7077888 | tf_op jit(solution)/shard_map/all_gather | solution.py:55
  505.5 54.7 %copy-start.3 = (f32[1024]{0:T(1024)S(1)}, f32[1024]{0:T(1024)}, u32[]{:S(2)}) copy-start(f32[1024]{0:T(1024)} %param.15) | copy-start | bytes 12292
Sparse Core Ops, SparseCore 0:
  308.0 97.6 all-gather.2
  407.7 97.6 all-gather.4
where the time goes:
time: 570 us; the launch traced here: 568 us
  local copies, waits for them, and re-layouts  294 us (52%)
  waiting for transfers between devices  193 us (34%)
  matrix products  37.7 us (7%)
  other arithmetic  14.4 us (3%)
  between operations  13.6 us (2%)
  blocking collectives  6.84 us (1%)
    gather x2, local copies, waits for them, and re-layouts, filter_all(): upper = jnp.where(lag_table < 0, filters[:, :, upper_idx], 0.0)  130 us
    gather x2, local copies, waits for them, and re-layouts, filter_all(): lower = jnp.where(lag_table >= 0, filters[:, :, lower_idx], 0.0)  130 us
    all_gather x1, waiting for transfers between devices, attend(): value_piece = lax.all_gather(valued, 'ctx', axis=0, tiled=True)  99.8 us
    all_gather x1, waiting for transfers between devices, attend(): key_piece = lax.all_gather(keyed, 'ctx', axis=0, tiled=True)  93.6 us
    dot_general x6, matrix products, update_block(): jnp.einsum('hsk,khd->shd', weights.astype(jnp.bfloat16), value_block, pre...  14.9 us
  transfers between devices with their start and end apart: 3, of which 2 were waited for; matrix products, arithmetic and copies ran while one was open for 47% of the time, Pallas kernels for 0%

commit v1 on v0

--- a/solution.py
+++ b/solution.py
@@ -52,7 +52,18 @@
         jnp.zeros((tok_rows, head_count, HD), jnp.float32),
     )
     key_piece = lax.all_gather(keyed, "ctx", axis=0, tiled=True)
-    value_piece = lax.all_gather(valued, "ctx", axis=0, tiled=True)
+    stack_in = [valued]
+    axis_total = lax.axis_size("ctx")
+    for u in range(1, axis_total):
+        q_next = lax.ppermute(
+            stack_in[u - 1],
+            axis_name="ctx",
+            perm=[(h, (h - 1) % axis_total) for h in range(axis_total)],
+        )
+        stack_in.append(q_next)
+    z1 = jnp.concatenate(stack_in, axis=0)
+    main = lax.axis_index("ctx")
+    value_piece = jnp.roll(z1, main * valued.shape[0], 0)
     piece_len = key_piece.shape[0]
     block_len = math.gcd(piece_len, 512)
 

time: 570 us -> 602 us (1.056)
  local copies, waits for them, and re-layouts: 294 us -> 326 us
  waiting for transfers between devices: 193 us -> 174 us
  starting transfers between devices: 3.65 us -> 21.4 us
    ppermute x0 -> x7, waiting for transfers between devices: none -> 174 us  [attend(): lax.ppermute(stack_in[u - 1], axis_name='ctx', perm=[(h, (h - 1) % axis_t...]
    all_gather x1 -> x0, waiting for transfers between devices: 99.8 us -> none  [attend(): value_piece = lax.all_gather(valued, 'ctx', axis=0, tiled=True)]
    all_gather x1, waiting for transfers between devices: 93.6 us -> 0.01 us  [attend(): key_piece = lax.all_gather(keyed, 'ctx', axis=0, tiled=True)]
    unnamed x20 -> x46, local copies, waits for them, and re-layouts: 3.46 us -> 26.9 us
    ppermute x0 -> x7, starting transfers between devices: none -> 17.9 us  [attend(): lax.ppermute(stack_in[u - 1], axis_name='ctx', perm=[(h, (h - 1) % axis_t...]
    dynamic_slice x0 -> x1, local copies, waits for them, and re-layouts: none -> 8.63 us  [attend(): value_piece = jnp.roll(z1, main * valued.shape[0], 0)]
  transfers between devices with their start and end apart: 3 -> 9, of which waited for: 2 -> 7; matrix products, arithmetic and copies ran while one was open for 47% -> 50% of each run, Pallas kernels for 0% -> 0%
where the time goes in v1:
time: 602 us; the launch traced here: 597 us
  local copies, waits for them, and re-layouts  326 us (54%)
  waiting for transfers between devices  174 us (29%)
  matrix products  37.7 us (6%)
  starting transfers between devices  21.4 us (4%)
  other arithmetic  14.4 us (2%)
  between operations  13.6 us (2%)
    ppermute x7, waiting for transfers between devices, attend(): lax.ppermute(stack_in[u - 1], axis_name='ctx', perm=[(h, (h - 1) % axis_t...  174 us
    gather x2, local copies, waits for them, and re-layouts, filter_all(): upper = jnp.where(lag_table < 0, filters[:, :, upper_idx], 0.0)  130 us
    gather x2, local copies, waits for them, and re-layouts, filter_all(): lower = jnp.where(lag_table >= 0, filters[:, :, lower_idx], 0.0)  129 us
    unnamed x46, local copies, waits for them, and re-layouts  26.9 us
    ppermute x7, starting transfers between devices, attend(): lax.ppermute(stack_in[u - 1], axis_name='ctx', perm=[(h, (h - 1) % axis_t...  17.9 us
    dot_general x6, matrix products, update_block(): jnp.einsum('hsk,khd->shd', weights.astype(jnp.bfloat16), value_block, pre...  14.9 us
  transfers between devices with their start and end apart: 9, of which 7 were waited for; matrix products, arithmetic and copies ran while one was open for 50% of the time, Pallas kernels for 0%

profile of v1, /device:TPU:24, one launch (start us, length us, event | category | flops | bytes accessed | tf_op | source)
XLA Modules:
  0.0 597.2 jit_solution(15262117205556679872)
XLA Ops:
  7.7 3.4 collective-permute-start
  13.0 112.3 %gather_fusion.1 = bf16[16384,3,64]{2,1,0:T(4,128)(2,1)} fusion(bf16[3,64,128]{1,0,2:T(4,128)(2,1)S(1)} %copy.17, s32[16384]{0:T(1024)S(1)} %broadcast_clamp_fusion), kind=kCustom, calls=%fused_computation.1 | custom fusion | bytes 12648448 | tf_op jit(solution)/shard_map/gather | solution.py:33
  125.2 17.3 %copy.21 = bf16[128,128,3,64]{1,0,3,2:T(8,128)(2,1)} copy(bf16[128,128,3,64]{3,2,1,0:T(4,128)(2,1)} %bitcast.81) | data formatting | bytes 12582912 | tf_op jit(solution)/shard_map/gather | solution.py:33
  142.5 112.1 %gather_fusion = bf16[16384,3,64]{2,1,0:T(4,128)(2,1)} fusion(bf16[3,64,128]{1,0,2:T(4,128)(2,1)S(1)} %copy.17, s32[16384]{0:T(1024)S(1)} %broadcast_clamp_fusion.1), kind=kCustom, calls=%fused_computation | custom fusion | bytes 12648448 | tf_op jit(solution)/shard_map/gather | solution.py:32
  254.6 17.2 %copy.18 = bf16[128,128,3,64]{1,0,3,2:T(8,128)(2,1)} copy(bf16[128,128,3,64]{3,2,1,0:T(4,128)(2,1)} %bitcast.80) | data formatting | bytes 12582912 | tf_op jit(solution)/shard_map/gather | solution.py:32
  271.8 2.1 pad_maximum_fusion
  273.9 2.9 copy.15
  276.9 5.6 reshape.74
  282.5 8.1 %fusion.40 = (bf16[3,3,128,64,16]{2,1,4,3,0:T(4,128)(2,1)}, bf16[3,3,128,64,16]{2,1,4,3,0:T(4,128)(2,1)S(1)}) fusion(bf16[3,4,128,64,16]{2,1,4,3,0:T(4,128)(2,1)} %reshape.74), kind=kLoop, calls=%fused_computation.73 | loop fusion | bytes 9437184 | tf_op jit(solution)/shard_map/slice | solution.py:35
  290.6 6.0 %fusion.18 = f32[3,64,3,16,128]{4,3,2,1,0:T(8,128)} fusion(bf16[128,128,3,64]{1,0,3,2:T(8,128)(2,1)S(1)} %bitcast.79, pred[128,128]{1,0:T(8,128)(4,1)S(1)} %bitcast.88, bf16[3,3,128,64,16]{2,1,4,3,0:T(4,128)(2,1)S(1)} %get-tuple-element.353), kind=kOutput, calls=%fused_computation.26 | convolution fusion | flops 305135616 | bytes 13385728 | tf_op jit(solution)/shard_map/agts,absgc->abtgc/dot_general | solution.py:37
  296.7 7.8 %fusion.28 = bf16[3,3,128,64,16]{2,4,1,3,0:T(8,128)(2,1)S(1)} fusion(f32[3,64,3,16,128]{4,3,2,1,0:T(8,128)} %fusion.18, bf16[128,128,3,64]{1,0,3,2:T(8,128)(2,1)S(1)} %bitcast.77, pred[128,128]{1,0:T(8,128)(4,1)S(1)} %bitcast.87, bf16[3,3,128,64,16]{2,1,4,3,0:T(4,128)(2,1)} %get-tuple-element.352), kind=kOutput, calls=%fused_computation.38 | convolution fusion | flops 307494912 | bytes 15745024 | tf_op jit(solution)/shard_map/agts,absgc->abtgc/dot_general | solution.py:34
  309.6 26.0 %collective-permute-done.1 = bf16[384,1024]{0,1:T(8,128)(2,1)S(1)} collective-permute-done((bf16[384,1024]{0,1:T(8,128)(2,1)S(1)}, bf16[384,1024]{0,1:T(8,128)(2,1)S(1)}, u32[]{:S(2)}, u32[]{:S(2)}) %collective-permute-start.1) | collective-permute-done | bytes 786464 | tf_op jit(solution)/shard_map/ppermute | solution.py:58
  335.6 2.3 collective-permute-start.2
  337.9 30.9 %collective-permute-done.2 = bf16[384,1024]{0,1:T(8,128)(2,1)S(1)} collective-permute-done((bf16[384,1024]{0,1:T(8,128)(2,1)S(1)}, bf16[384,1024]{0,1:T(8,128)(2,1)S(1)}, u32[]{:S(2)}, u32[]{:S(2)}) %collective-permute-start.2) | collective-permute-done | bytes 786464 | tf_op jit(solution)/shard_map/ppermute | solution.py:58
  368.8 3.4 collective-permute-start.3
  372.2 32.1 %collective-permute-done.3 = bf16[384,1024]{0,1:T(8,128)(2,1)S(1)} collective-permute-done((bf16[384,1024]{0,1:T(8,128)(2,1)S(1)}, bf16[384,1024]{0,1:T(8,128)(2,1)S(1)}, u32[]{:S(2)}, u32[]{:S(2)}) %collective-permute-start.3) | collective-permute-done | bytes 786464 | tf_op jit(solution)/shard_map/ppermute | solution.py:58
  405.2 3.4 collective-permute-start.4
  408.6 30.9 %collective-permute-done.4 = bf16[384,1024]{0,1:T(8,128)(2,1)S(1)} collective-permute-done((bf16[384,1024]{0,1:T(8,128)(2,1)S(1)}, bf16[384,1024]{0,1:T(8,128)(2,1)S(1)}, u32[]{:S(2)}, u32[]{:S(2)}) %collective-permute-start.4) | collective-permute-done | bytes 786464 | tf_op jit(solution)/shard_map/ppermute | solution.py:58
  440.4 3.4 collective-permute-start.5
  443.8 28.6 %collective-permute-done.5 = bf16[384,1024]{0,1:T(8,128)(2,1)} collective-permute-done((bf16[384,1024]{0,1:T(8,128)(2,1)S(1)}, bf16[384,1024]{0,1:T(8,128)(2,1)}, u32[]{:S(2)}, u32[]{:S(2)}) %collective-permute-start.5) | collective-permute-done | bytes 786464 | tf_op jit(solution)/shard_map/ppermute | solution.py:58
  472.4 3.5 collective-permute-start.6
  478.3 16.2 %collective-permute-done.6 = bf16[384,1024]{0,1:T(8,128)(2,1)} collective-permute-done((bf16[384,1024]{0,1:T(8,128)(2,1)}, bf16[384,1024]{0,1:T(8,128)(2,1)}, u32[]{:S(2)}, u32[]{:S(2)}) %collective-permute-start.6) | collective-permute-done | bytes 786464 | tf_op jit(solution)/shard_map/ppermute | solution.py:58
  497.0 2.2 constant_dynamic-update-slice_fusion.12
  499.3 2.3 constant_dynamic-update-slice_fusion.11
  501.5 2.2 constant_dynamic-update-slice_fusion.10
  503.7 2.3 constant_dynamic-update-slice_fusion.9
  506.0 8.8 %collective-permute-done.7 = bf16[384,1024]{0,1:T(8,128)(2,1)S(1)} collective-permute-done((bf16[384,1024]{0,1:T(8,128)(2,1)}, bf16[384,1024]{0,1:T(8,128)(2,1)S(1)}, u32[]{:S(2)}, u32[]{:S(2)}) %collective-permute-start.7) | collective-permute-done | bytes 786464 | tf_op jit(solution)/shard_map/ppermute | solution.py:58
  521.1 2.1 constant_dynamic-update-slice_fusion.2
  523.3 2.2 constant_dynamic-update-slice_fusion.1
  526.5 8.6 %constant_dynamic-slice_fusion.2 = bf16[3072,1024]{0,1:T(8,128)(2,1)} fusion(bf16[6144,1024]{0,1:T(8,128)(2,1)} %constant_dynamic-update-slice_fusion, s32[]{:T(128)S(6)} %select_n.54), kind=kLoop, calls=%fused_computation.70 | loop fusion | bytes 12582916 | tf_op jit(solution)/shard_map/jit(_roll_dynamic)/dynamic_slice | solution.py:66
  535.3 47.7 %while.18 = (s32[]{:T(128)}, f32[8,384]{1,0:T(8,128)S(1)}, f32[8,384]{1,0:T(8,128)S(1)}, f32[384,8,128]{2,0,1:T(8,128)S(1)}, s32[]{:T(128)}, /*index=5*/bf16[307...) while((s32[]{:T(128)}, f32[8,384]{1,0:T(8,128)S(1)}, ...), condition=%wide.region_6.7_spmd.clone, body=%wide.region_1.6_spmd.clone.sunk | while | flops 823601024 | bytes 30095668 | solution.py:103
  536.0 7.3 %conditional.3 = (f32[8,384]{1,0:T(8,128)S(1)}, f32[8,384]{1,0:T(8,128)S(1)}, f32[384,8,128]{2,0,1:T(8,128)S(1)}) conditional(s32[]{:T(128)} %convert_element_type.65, (s32[]{:T(128)}, s32[512]{0:T(512)S(1)}, s32[]{:T(128)}, bf16[3072,1024]{0,1:T(8,128)(2,1)}, bf16[384,8,128]{2,0,1:T(8,128)(2,1)S(1)}, /*index=5*/f32[8,384]{1,0:T(8,128)S(1)}, ...), branch_computations={%region_2.4_spmd, %region_5.5_spmd} | conditional | flops 823601024 | bytes 30067270 | solution.py:101
  536.0 1.7 constant_dynamic-slice_fusion
  539.4 2.5 bitcast_add_fusion
  543.9 7.3 %conditional.3 = (f32[8,384]{1,0:T(8,128)S(1)}, f32[8,384]{1,0:T(8,128)S(1)}, f32[384,8,128]{2,0,1:T(8,128)S(1)}) conditional(s32[]{:T(128)} %convert_element_type.65, (s32[]{:T(128)}, s32[512]{0:T(512)S(1)}, s32[]{:T(128)}, bf16[3072,1024]{0,1:T(8,128)(2,1)}, bf16[384,8,128]{2,0,1:T(8,128)(2,1)S(1)}, /*index=5*/f32[8,384]{1,0:T(8,128)S(1)}, ...), branch_computations={%region_2.4_spmd, %region_5.5_spmd} | conditional | flops 823601024 | bytes 30067270 | solution.py:101
  543.9 1.7 constant_dynamic-slice_fusion
  547.4 2.5 bitcast_add_fusion
  551.9 7.3 %conditional.3 = (f32[8,384]{1,0:T(8,128)S(1)}, f32[8,384]{1,0:T(8,128)S(1)}, f32[384,8,128]{2,0,1:T(8,128)S(1)}) conditional(s32[]{:T(128)} %convert_element_type.65, (s32[]{:T(128)}, s32[512]{0:T(512)S(1)}, s32[]{:T(128)}, bf16[3072,1024]{0,1:T(8,128)(2,1)}, bf16[384,8,128]{2,0,1:T(8,128)(2,1)S(1)}, /*index=5*/f32[8,384]{1,0:T(8,128)S(1)}, ...), branch_computations={%region_2.4_spmd, %region_5.5_spmd} | conditional | flops 823601024 | bytes 30067270 | solution.py:101
  555.3 2.5 bitcast_add_fusion
  559.8 7.3 %conditional.3 = (f32[8,384]{1,0:T(8,128)S(1)}, f32[8,384]{1,0:T(8,128)S(1)}, f32[384,8,128]{2,0,1:T(8,128)S(1)}) conditional(s32[]{:T(128)} %convert_element_type.65, (s32[]{:T(128)}, s32[512]{0:T(512)S(1)}, s32[]{:T(128)}, bf16[3072,1024]{0,1:T(8,128)(2,1)}, bf16[384,8,128]{2,0,1:T(8,128)(2,1)S(1)}, /*index=5*/f32[8,384]{1,0:T(8,128)S(1)}, ...), branch_computations={%region_2.4_spmd, %region_5.5_spmd} | conditional | flops 823601024 | bytes 30067270 | solution.py:101
  559.8 1.7 constant_dynamic-slice_fusion
  563.3 2.5 bitcast_add_fusion
  567.8 7.3 %conditional.3 = (f32[8,384]{1,0:T(8,128)S(1)}, f32[8,384]{1,0:T(8,128)S(1)}, f32[384,8,128]{2,0,1:T(8,128)S(1)}) conditional(s32[]{:T(128)} %convert_element_type.65, (s32[]{:T(128)}, s32[512]{0:T(512)S(1)}, s32[]{:T(128)}, bf16[3072,1024]{0,1:T(8,128)(2,1)}, bf16[384,8,128]{2,0,1:T(8,128)(2,1)S(1)}, /*index=5*/f32[8,384]{1,0:T(8,128)S(1)}, ...), branch_computations={%region_2.4_spmd, %region_5.5_spmd} | conditional | flops 823601024 | bytes 30067270 | solution.py:101
  571.2 2.5 bitcast_add_fusion
  575.7 7.3 %conditional.3 = (f32[8,384]{1,0:T(8,128)S(1)}, f32[8,384]{1,0:T(8,128)S(1)}, f32[384,8,128]{2,0,1:T(8,128)S(1)}) conditional(s32[]{:T(128)} %convert_element_type.65, (s32[]{:T(128)}, s32[512]{0:T(512)S(1)}, s32[]{:T(128)}, bf16[3072,1024]{0,1:T(8,128)(2,1)}, bf16[384,8,128]{2,0,1:T(8,128)(2,1)S(1)}, /*index=5*/f32[8,384]{1,0:T(8,128)S(1)}, ...), branch_computations={%region_2.4_spmd, %region_5.5_spmd} | conditional | flops 823601024 | bytes 30067270 | solution.py:101
  575.7 1.7 constant_dynamic-slice_fusion
  579.2 2.5 bitcast_add_fusion
  583.6 5.7 psum.7
  (126 shorter events, 45.4 us)
Async XLA Ops:
  6.5 528.6 %all-gather.2.cloned.1.call-start = ((), (), s32[]{:S(2)}) async-start(), calls=%async_computation | async-start | bytes 7077888 | tf_op jit(solution)/shard_map/all_gather | solution.py:54
  7.7 264.1 %collective-permute-start = (bf16[3,128,1024]{2,1,0:T(8,128)(2,1)S(1)}, bf16[3,128,1024]{2,1,0:T(8,128)(2,1)}, u32[]{:S(2)}, u32[]{:S(2)}) collective-permute-start(bf16[3,128,1024]{2,1,0:T(8,128)(2,1)S(1)} %slice.21), channel_id=1, source_target_pairs={{0,4},{4,8},{8,12},{12,16},{16,20},{20,24},{24,28},{1,5},{5,9},{9,... | collective-permute-start | bytes 2359304 | tf_op jit(solution)/shard_map/ppermute | solution.py:15
  125.2 17.3 %copy-start.8 = (s32[16384]{0:T(1024)S(1)}, s32[16384]{0:T(1024)}, u32[]{:S(2)}) copy-start(s32[16384]{0:T(1024)} %constant.121) | copy-start | bytes 196612
  276.9 13.7 %slice-start.2 = ((s8[6291456]{0:T(1024)(128)(4,1)}), s8[2097152]{0:T(1024)(128)(4,1)S(1)}, s32[]{:S(2)}) async-start(s8[6291456]{0:T(1024)(128)(4,1)} %bitcast.78), calls=%async_computation.3 | async-start | bytes 4194304
  282.5 8.1 %slice-start.3 = ((s8[6291456]{0:T(1024)(128)(4,1)}), s8[4194304]{0:T(1024)(128)(4,1)S(1)}, s32[]{:S(2)}) async-start(s8[6291456]{0:T(1024)(128)(4,1)} %bitcast.78), calls=%async_computation.4 | async-start | bytes 8388608
  282.5 8.1 %copy-start.7 = (pred[128,128]{1,0:T(32,128)(4,1)S(1)}, pred[128,128]{1,0:T(32,128)(4,1)}, u32[]{:S(2)}) copy-start(pred[128,128]{1,0:T(32,128)(4,1)} %constant.118.clone) | copy-start | bytes 49156
  282.5 14.2 %slice-start = ((s8[6291456]{0:T(1024)(128)(4,1)}), s8[4194304]{0:T(1024)(128)(4,1)S(1)}, s32[]{:S(2)}) async-start(s8[6291456]{0:T(1024)(128)(4,1)} %bitcast.76), calls=%async_computation.1 | async-start | bytes 8388608
  290.6 6.1 %slice-start.1 = ((s8[6291456]{0:T(1024)(128)(4,1)}), s8[2097152]{0:T(1024)(128)(4,1)S(1)}, s32[]{:S(2)}) async-start(s8[6291456]{0:T(1024)(128)(4,1)} %bitcast.76), calls=%async_computation.2 | async-start | bytes 4194304
  290.6 6.1 %copy-start.6 = (pred[128,128]{1,0:T(32,128)(4,1)S(1)}, pred[128,128]{1,0:T(32,128)(4,1)}, u32[]{:S(2)}) copy-start(pred[128,128]{1,0:T(32,128)(4,1)} %constant.116.clone) | copy-start | bytes 49156
  308.2 164.2 %copy-start.4 = (bf16[384,1024]{0,1:T(8,128)(2,1)}, bf16[384,1024]{0,1:T(8,128)(2,1)S(1)}, u32[]{:S(2)}) copy-start(bf16[384,1024]{0,1:T(8,128)(2,1)S(1)} %get-tuple-element.347) | copy-start | bytes 2359300
  308.2 27.4 %collective-permute-start.1 = (bf16[384,1024]{0,1:T(8,128)(2,1)S(1)}, bf16[384,1024]{0,1:T(8,128)(2,1)S(1)}, u32[]{:S(2)}, u32[]{:S(2)}) collective-permute-start(bf16[384,1024]{0,1:T(8,128)(2,1)S(1)} %get-tuple-element.347), channel_id=1, source_target_pairs={{0,28},{4,0},{8,4},{12,8},{16,12},{20,16},{24,20},{28,24},{1,29},{... | collective-permute-start | bytes 2359304 | tf_op jit(solution)/shard_map/ppermute | solution.py:58
  335.6 33.2 %collective-permute-start.2 = (bf16[384,1024]{0,1:T(8,128)(2,1)S(1)}, bf16[384,1024]{0,1:T(8,128)(2,1)S(1)}, u32[]{:S(2)}, u32[]{:S(2)}) collective-permute-start(bf16[384,1024]{0,1:T(8,128)(2,1)S(1)} %collective-permute-done.1), channel_id=1, source_target_pairs={{0,28},{4,0},{8,4},{12,8},{16,12},{20,16},{24,20},{28,24},{1,29},{... | collective-permute-start | bytes 2359304 | tf_op jit(solution)/shard_map/ppermute | solution.py:58
  368.8 35.5 %collective-permute-start.3 = (bf16[384,1024]{0,1:T(8,128)(2,1)S(1)}, bf16[384,1024]{0,1:T(8,128)(2,1)S(1)}, u32[]{:S(2)}, u32[]{:S(2)}) collective-permute-start(bf16[384,1024]{0,1:T(8,128)(2,1)S(1)} %collective-permute-done.2), channel_id=1, source_target_pairs={{0,28},{4,0},{8,4},{12,8},{16,12},{20,16},{24,20},{28,24},{1,29},{... | collective-permute-start | bytes 2359304 | tf_op jit(solution)/shard_map/ppermute | solution.py:58
  404.3 0.9 copy-start
  405.2 34.3 %collective-permute-start.4 = (bf16[384,1024]{0,1:T(8,128)(2,1)S(1)}, bf16[384,1024]{0,1:T(8,128)(2,1)S(1)}, u32[]{:S(2)}, u32[]{:S(2)}) collective-permute-start(bf16[384,1024]{0,1:T(8,128)(2,1)S(1)} %collective-permute-done.3), channel_id=1, source_target_pairs={{0,28},{4,0},{8,4},{12,8},{16,12},{20,16},{24,20},{28,24},{1,29},{... | collective-permute-start | bytes 2359304 | tf_op jit(solution)/shard_map/ppermute | solution.py:58
  439.5 0.9 copy-start.2
  440.4 32.0 %collective-permute-start.5 = (bf16[384,1024]{0,1:T(8,128)(2,1)S(1)}, bf16[384,1024]{0,1:T(8,128)(2,1)}, u32[]{:S(2)}, u32[]{:S(2)}) collective-permute-start(bf16[384,1024]{0,1:T(8,128)(2,1)S(1)} %collective-permute-done.4), channel_id=1, source_target_pairs={{0,28},{4,0},{8,4},{12,8},{16,12},{20,16},{24,20},{28,24},{1,29},{... | collective-permute-start | bytes 2359304 | tf_op jit(solution)/shard_map/ppermute | solution.py:58
  472.4 22.1 %collective-permute-start.6 = (bf16[384,1024]{0,1:T(8,128)(2,1)}, bf16[384,1024]{0,1:T(8,128)(2,1)}, u32[]{:S(2)}, u32[]{:S(2)}) collective-permute-start(bf16[384,1024]{0,1:T(8,128)(2,1)} %collective-permute-done.5), channel_id=1, source_target_pairs={{0,28},{4,0},{8,4},{12,8},{16,12},{20,16},{24,20},{28,24},{1,29},{... | collective-permute-start | bytes 2359304 | tf_op jit(solution)/shard_map/ppermute | solution.py:58
  478.2 37.6 %copy-start.5 = (bf16[384,1024]{0,1:T(8,128)(2,1)S(1)}, bf16[384,1024]{0,1:T(8,128)(2,1)}, u32[]{:S(2)}) copy-start(bf16[384,1024]{0,1:T(8,128)(2,1)} %copy-done.4) | copy-start | bytes 2359300
  494.5 20.3 %collective-permute-start.7 = (bf16[384,1024]{0,1:T(8,128)(2,1)}, bf16[384,1024]{0,1:T(8,128)(2,1)S(1)}, u32[]{:S(2)}, u32[]{:S(2)}) collective-permute-start(bf16[384,1024]{0,1:T(8,128)(2,1)} %collective-permute-done.6), channel_id=1, source_target_pairs={{0,28},{4,0},{8,4},{12,8},{16,12},{20,16},{24,20},{28,24},{1,29},{... | collective-permute-start | bytes 2359304 | tf_op jit(solution)/shard_map/ppermute | solution.py:58
  497.0 22.0 %copy-start.1 = (bf16[384,1024]{0,1:T(8,128)(2,1)S(1)}, bf16[384,1024]{0,1:T(8,128)(2,1)}, u32[]{:S(2)}) copy-start(bf16[384,1024]{0,1:T(8,128)(2,1)} %copy-done) | copy-start | bytes 2359300
  499.3 20.8 %copy-start.3 = (bf16[384,1024]{0,1:T(8,128)(2,1)S(1)}, bf16[384,1024]{0,1:T(8,128)(2,1)}, u32[]{:S(2)}) copy-start(bf16[384,1024]{0,1:T(8,128)(2,1)} %copy-done.2) | copy-start | bytes 2359300
  535.3 54.0 %copy-start.9 = (f32[1024]{0:T(1024)S(1)}, f32[1024]{0:T(1024)}, u32[]{:S(2)}) copy-start(f32[1024]{0:T(1024)} %param.15) | copy-start | bytes 12292
Sparse Core Ops, SparseCore 0:
  306.6 170.1 all-gather.1
